TPU v7x, 256 devices: a whole 4x4x8 slice. The times are simulated.
256 devices in a mesh: graph: 64 (over x, z, core), rep: 4 (over y).
Axes of the slice: x: 4, y: 4, z: 8, core: 2. Of those that a mesh axis runs over, the one named last changes fastest.
Arguments:
- node_feats: bfloat16 [4, 1024, 49, 256], P('rep', 'graph'), may hold values from -6 to 6
- species: int32 [4, 1024], P('rep', 'graph'), may hold values from 0 to 89
- charge: int32 [4], P('rep'), may hold values from 0 to 8
- species_table: float32 [90, 256], replicated, may hold values from -6 to 6
- charge_table: float32 [9, 256], replicated, may hold values from -6 to 6
- so2_weight: bfloat16 [1792, 1792], replicated, may hold values from -0.125 to 0.125
- edge_frame: bfloat16 [4, 49, 16384], P('rep', None, 'graph'), as said below
- edge_src: int32 [4, 16384], P('rep', 'graph'), may hold values from 0 to 1023, as said below
- edge_dst: int32 [4, 16384], P('rep', 'graph'), may hold values from 0 to 1023, as said below
- edge_count: int32 [4, 64], P('rep', 'graph'), may hold values from 32 to 192, as said below
- out_cotangent: bfloat16 [4, 1024, 49, 256], P('rep', 'graph'), may hold values from -6 to 6
Outputs:
- updated_feats: bfloat16 [4, 1024, 49, 256], P('rep', 'graph')
- feat_grad: bfloat16 [4, 1024, 49, 256], P('rep', 'graph')
- weight_grad: float32 [3211264], P(('graph', 'rep'))
- species_grad: float32 [90, 256], replicated
- charge_grad: float32 [9, 256], replicated
Inputs may be any that keep to these rules, and one draw needn't show every extreme that they name: `edge_count`: live slots of one device per cell. Two devices whose graph indices differ by half the axis hold at most 256 live slots together; in every cell some device holds exactly 192. `edge_src`: in a live slot the source atom's device (index // 16) is at most 2 devices from the slot's device along graph, cyclically; a slot that is not live holds its device's first atom. `edge_dst`: each slot's destination atom belongs to the device that holds the slot; a slot that is not live holds its device's first atom. `edge_frame`: for every edge and degree l the 2l+1 entries of degree l have unit sum of squares; the degree-0 entry is 1.
All inputs are finite; a program needn't handle non-finite values.
Results may differ from a plain program's by a relative error of at most 0.0066.
Values may be sent and summed in bfloat16 or wider, within the bound.
No kernel may reach another device: no remote copies, remote signals or barrier semaphores. Data moves between devices by JAX's collectives and lax.ppermute only.
A program may use at most 128 MiB of HBM per device.

v0:
```python
import jax
import jax.numpy as jnp
from jax import lax
from jax.sharding import PartitionSpec as P

LMAX = 6
SPECIES = 90
CHARGES = 9
REACH = 2


MSG_SCALE = 0.25
PRECISE = lax.Precision.HIGHEST


def from_behind(block, axis, distance):
    devices = range(lax.axis_size(axis))
    route = [((i - distance) % len(devices), i) for i in devices]
    return lax.ppermute(block, axis, route)


def degree_spans():
    return [(degree * degree, (degree + 1) * (degree + 1)) for degree in range(LMAX + 1)]


def gate_forward(pre_act):
    return pre_act * jax.nn.sigmoid(pre_act[:, :1, :])


def gate_backward(pre_act, grad_out):
    sig_gate = jax.nn.sigmoid(pre_act[:, :1, :])
    cross_term = jnp.sum(grad_out * pre_act, axis=1, keepdims=True) * sig_gate * (1.0 - sig_gate)
    scaled = grad_out * sig_gate
    return jnp.concatenate([scaled[:, :1, :] + cross_term, scaled[:, 1:, :]], axis=1)


def gate_rows(pre_act):
    row_count = pre_act.shape[0]
    return gate_forward(pre_act.reshape(row_count, LMAX + 1, -1)).reshape(row_count, -1)


def gate_rows_back(pre_act, grad_out):
    row_count = pre_act.shape[0]
    shaped = gate_backward(
        pre_act.reshape(row_count, LMAX + 1, -1), grad_out.reshape(row_count, LMAX + 1, -1)
    )
    return shaped.reshape(row_count, -1)


def contract_rows(left_mat, right_mat):
    return lax.dot_general(
        left_mat, right_mat, (((0,), (0,)), ((), ())), preferred_element_type=jnp.float32
    )


def edge_coefs(onehot, frame_rows):
    return (onehot[:, :, None] * jnp.transpose(frame_rows)[:, None, :]).reshape(onehot.shape[0], -1)


def local(
    node_feats,
    species,
    charge,
    species_table,
    charge_table,
    so2_weight,
    edge_frame,
    edge_src,
    edge_dst,
    edge_count,
    out_cotangent,
):
    atoms_here = node_feats.shape[1]
    coef_count = node_feats.shape[2]
    channels = node_feats.shape[3]
    edges_here = edge_src.shape[1]
    graph_size = lax.axis_size("graph")
    graph_pos = lax.axis_index("graph")
    live_count = edge_count[0, 0]
    features = node_feats[0].astype(jnp.float32)
    spec_hot = (species[0][:, None] == jnp.arange(SPECIES, dtype=jnp.int32)[None, :]).astype(
        jnp.float32
    )
    charge_hot = (jnp.arange(CHARGES, dtype=jnp.int32) == charge[0]).astype(jnp.float32)
    embedding = (
        jnp.dot(spec_hot, species_table, precision=PRECISE)
        + jnp.dot(charge_hot, charge_table, precision=PRECISE)[None, :]
    )
    hidden = jnp.concatenate(
        [features[:, :1, :] + embedding[:, None, :], features[:, 1:, :]], axis=1
    ).astype(jnp.bfloat16)
    blocks = []
    for offset in range(-REACH, REACH + 1):
        if offset == 0:
            blocks.append(hidden)
        else:
            blocks.append(from_behind(hidden, "graph", -offset))
    block_total = len(blocks)
    nearby = jnp.stack(blocks, axis=0).reshape(block_total * atoms_here, coef_count, channels)
    sources = edge_src[0]
    targets = edge_dst[0]
    slot_ids = jnp.arange(edges_here, dtype=jnp.int32)
    live_mask = slot_ids < live_count
    rel_owner = (sources // atoms_here - graph_pos + REACH) % graph_size
    local_src = rel_owner * atoms_here + sources % atoms_here
    src_hot = (
        (local_src[:, None] == jnp.arange(block_total * atoms_here, dtype=jnp.int32)[None, :])
        & live_mask[:, None]
    ).astype(jnp.bfloat16)
    local_dst = targets - graph_pos * atoms_here
    dst_hot = (
        (local_dst[:, None] == jnp.arange(atoms_here, dtype=jnp.int32)[None, :])
        & live_mask[:, None]
    ).astype(jnp.bfloat16)
    frame_all = edge_frame[0]
    src_coefs = []
    dst_coefs = []
    rotated_pieces = []
    for lower_k, upper_k in degree_spans():
        frame_rows = frame_all[lower_k:upper_k]
        src_coef = edge_coefs(src_hot, frame_rows)
        src_coefs.append(src_coef)
        dst_coefs.append(edge_coefs(dst_hot, frame_rows))
        node_piece = nearby[:, lower_k:upper_k, :].reshape(-1, channels)
        rotated_pieces.append(jnp.dot(src_coef, node_piece, preferred_element_type=jnp.float32))
    rotated = jnp.concatenate(rotated_pieces, axis=1).astype(jnp.bfloat16)
    pre_act = jnp.dot(rotated, so2_weight, preferred_element_type=jnp.float32)
    gated = gate_rows(pre_act).astype(jnp.bfloat16)
    agg_pieces = []
    grad_pieces = []
    cotangent = out_cotangent[0]
    for degree, (lower_k, upper_k) in enumerate(degree_spans()):
        value_piece = gated[:, degree * channels : (degree + 1) * channels]
        agg_pieces.append(
            contract_rows(dst_coefs[degree], value_piece).reshape(
                atoms_here, upper_k - lower_k, channels
            )
        )
        cot_piece = cotangent[:, lower_k:upper_k, :].reshape(-1, channels)
        grad_pieces.append(
            MSG_SCALE * jnp.dot(dst_coefs[degree], cot_piece, preferred_element_type=jnp.float32)
        )
    aggregate = jnp.concatenate(agg_pieces, axis=1)
    updated = (features + MSG_SCALE * aggregate).astype(jnp.bfloat16)
    grad_values = jnp.concatenate(grad_pieces, axis=1)
    grad_pre = gate_rows_back(pre_act, grad_values).astype(jnp.bfloat16)
    weight_part = contract_rows(rotated, grad_pre)
    work_rot = lax.dot_general(
        grad_pre, so2_weight, (((1,), (1,)), ((), ())), preferred_element_type=jnp.float32
    ).astype(jnp.bfloat16)
    node_pieces = []
    for degree, (lower_k, upper_k) in enumerate(degree_spans()):
        rot_piece = work_rot[:, degree * channels : (degree + 1) * channels]
        node_pieces.append(
            contract_rows(src_coefs[degree], rot_piece).reshape(
                block_total * atoms_here, upper_k - lower_k, channels
            )
        )
    node_terms = (
        jnp.concatenate(node_pieces, axis=1)
        .astype(jnp.bfloat16)
        .reshape(block_total, atoms_here, coef_count, channels)
    )
    grad_total = jnp.zeros((atoms_here, coef_count, channels), jnp.float32)
    for offset in range(-REACH, REACH + 1):
        grad_piece = node_terms[offset + REACH]
        if offset == 0:
            grad_total = grad_total + grad_piece.astype(jnp.float32)
        else:
            grad_total = grad_total + from_behind(grad_piece, "graph", offset).astype(jnp.float32)
    feat_grad = (cotangent.astype(jnp.float32) + grad_total).astype(jnp.bfloat16)
    invariant = grad_total[:, 0, :]
    species_part = jnp.dot(jnp.transpose(spec_hot), invariant, precision=PRECISE)
    charge_part = charge_hot[:, None] * jnp.sum(invariant, axis=0)[None, :]
    species_grad, charge_grad = lax.psum((species_part, charge_part), ("graph", "rep"))
    flat_grad = weight_part.reshape(-1)
    weight_grad = lax.psum_scatter(flat_grad, ("graph", "rep"), scatter_dimension=0, tiled=True)
    return (updated[None], feat_grad[None], weight_grad, species_grad, charge_grad)


def solution(mesh):
    in_specs = (
        P("rep", "graph", None, None),
        P("rep", "graph"),
        P("rep"),
        P(),
        P(),
        P(),
        P("rep", None, "graph"),
        P("rep", "graph"),
        P("rep", "graph"),
        P("rep", "graph"),
        P("rep", "graph", None, None),
    )
    out_specs = (
        P("rep", "graph", None, None),
        P("rep", "graph", None, None),
        P(("graph", "rep")),
        P(),
        P(),
    )
    return jax.shard_map(local, mesh=mesh, in_specs=in_specs, out_specs=out_specs, check_vma=False)
```

profile of v0, /device:TPU:8, one launch (start us, length us, event | category | flops | bytes accessed | tf_op | source)
XLA Modules:
  0.0 389.3 jit_solution(1866182456010812411)
XLA Ops:
  8.0 1.1 convert_bitcast_fusion
  9.2 0.8 fusion.118
  10.2 0.8 pad_maximum_fusion.1
  11.0 8.1 %collective-permute-start.3 = (bf16[16,49,256]{2,0,1:T(8,128)(2,1)}, bf16[16,49,256]{2,0,1:T(8,128)(2,1)}, u32[]{:S(2)}, u32[]{:S(2)}) collective-permute-start(bf16[16,49,256]{2,0,1:T(8,128)(2,1)} %pad_maximum_fusion.1), channel_id=1, source_target_pairs={{8,0},{12,4},{16,8},{20,12},{24,16},{28,20},{32,24},{36,28},{40,32... | collective-permute-start | bytes 1204232 | tf_op jit(solution)/shard_map/ppermute | solution.py:19
  19.2 0.3 collective-permute-start.1
  19.6 0.7 collective-permute-start
  20.4 0.6 slice.237
  21.0 0.6 slice.238
  21.6 0.6 slice.239
  23.1 0.6 broadcast_multiply_fusion.12
  24.2 0.7 dot_general.189
  25.0 0.8 dot_general.192
  25.9 0.8 dot_general.195
  27.0 1.0 dot_general.204
  28.3 1.0 dot_general.201
  29.5 1.0 dot_general.198
  30.5 0.2 fusion.5
  30.7 1.0 fusion.13
  31.8 0.2 fusion.15
  32.0 0.2 fusion.17
  32.2 1.1 fusion.7
  33.4 1.1 fusion.9
  34.5 1.1 fusion.11
  35.6 1.3 copy-done.3
  36.9 1.0 bitcast_dynamic-update-slice_fusion.3
  38.0 1.2 bitcast_dynamic-update-slice_fusion.2
  39.2 1.2 bitcast_dynamic-update-slice_fusion.1
  40.4 1.0 bitcast_dynamic-update-slice_fusion
  41.6 0.2 fusion.31
  42.0 0.3 copy-done.8
  42.4 0.3 fusion.22
  42.7 0.3 fusion.24
  43.0 0.4 fusion.30
  43.4 0.4 fusion.26
  43.8 0.4 fusion.28
  44.2 3.1 fusion.131
  47.3 2.9 copy.52
  50.2 1.0 fusion.85
  51.3 2.5 multiply_reduce_fusion
  53.9 1.0 fusion.58
  55.1 1.9 convolution_convert_fusion
  57.6 0.2 fusion.3
  58.1 0.3 fusion.2
  58.4 0.3 fusion.1
  58.7 0.3 fusion
  59.0 1.2 fusion.130
  60.2 4.7 %collective-permute-start.4 = (bf16[16,49,256]{2,0,1:T(8,128)(2,1)}, bf16[16,49,256]{2,0,1:T(8,128)(2,1)}, u32[]{:S(2)}, u32[]{:S(2)}) collective-permute-start(bf16[16,49,256]{2,0,1:T(8,128)(2,1)} %get-tuple-element.9), channel_id=1, source_target_pairs={{8,0},{12,4},{16,8},{20,12},{24,16},{28,20},{32,24},{36,28},{40,32... | collective-permute-start | bytes 1204232 | tf_op jit(solution)/shard_map/ppermute | solution.py:19
  64.9 0.2 collective-permute-start.6
  65.1 4.8 %collective-permute-start.5 = (bf16[16,49,256]{2,0,1:T(8,128)(2,1)}, bf16[16,49,256]{2,0,1:T(8,128)(2,1)}, u32[]{:S(2)}, u32[]{:S(2)}) collective-permute-start(bf16[16,49,256]{2,0,1:T(8,128)(2,1)} %get-tuple-element.12), channel_id=1, source_target_pairs={{4,0},{8,4},{12,8},{16,12},{20,16},{24,20},{28,24},{32,28},{36,32}... | collective-permute-start | bytes 1204232 | tf_op jit(solution)/shard_map/ppermute | solution.py:19
  69.9 6.5 %fusion.132 = f32[1792,1792]{1,0:T(8,128)} fusion(bf16[256,1792]{0,1:T(8,128)(2,1)S(1)} %fusion.28, bf16[256,1792]{0,1:T(8,128)(2,1)S(1)} %bitcast.274), kind=kOutput, calls=%fused_computation.227 | convolution fusion | flops 1644167168 | bytes 14680064 | tf_op jit(solution)/shard_map/dot_general | solution.py:51
  76.5 13.6 %reshape.520 = f32[3211264]{0:T(1024)} reshape(f32[1792,1792]{1,0:T(8,128)} %fusion.132) | data formatting | bytes 25690112 | tf_op jit(solution)/shard_map/reshape | solution.py:176
  90.1 2.4 fusion.51
  92.6 0.9 copy-done.11
  93.5 1.0 fusion.100
  94.5 0.7 copy-done.21
  95.9 1.4 mul.342
  97.2 2.9 copy.53
  100.2 2.2 multiply_convert_fusion
  103.6 0.9 fusion.44
  104.5 0.7 slice_reduce_fusion
  105.3 72.7 %psum.15 = f32[9,256]{1,0:T(8,128)} all-reduce(f32[9,256]{1,0:T(8,128)S(1)} %broadcast_multiply_fusion.16), channel_id=1, replica_groups=mesh['graph'=64,'rep'=4] {'graph','rep'}, use_global_device_ids=true, to_apply=%region_4.5 | all-reduce | flops 2304 | bytes 18432 | tf_op jit(solution)/shard_map/psum | solution.py:175
  178.0 201.4 %all-reduce.4.cloned.1.call-done = (f32[3211264]{0:T(1024)}, f32[90,256]{1,0:T(8,128)}) async-done(((f32[3211264]{0:T(1024)}, f32[90,256]{1,0:T(8,128)}), (f32[3211264]{0:T(1024)}, f32[90,256]{1,0:T(8,128)})) %all-reduce.4.cloned.1.call-update) | async-done | bytes 12937232
  379.4 1.5 dynamic-slice
  381.0 1.5 copy.152
  (151 shorter events, 5.1 us)
Async XLA Ops:
  7.2 2.8 copy-start
  7.2 2.8 copy-start.30
  7.2 13.1 %copy-start.25 = (bf16[1,49,256]{2,1,0:T(8,128)(2,1)S(1)}, bf16[1,49,256]{2,1,0:T(8,128)(2,1)}, u32[]{:S(2)}) copy-start(bf16[1,49,256]{2,1,0:T(8,128)(2,1)} %param.17) | copy-start | bytes 75268
  7.2 13.2 %copy-start.4 = (bf16[1,16,49,256]{3,1,2,0:T(8,128)(2,1)S(1)}, bf16[1,16,49,256]{3,1,2,0:T(8,128)(2,1)}, u32[]{:S(2)}) copy-start(bf16[1,16,49,256]{3,1,2,0:T(8,128)(2,1)} %param.21) | copy-start | bytes 1204228
  7.2 15.7 %copy-start.32 = (s32[1,256]{1,0:T(1,128)S(1)}, s32[1,256]{1,0:T(1,128)}, u32[]{:S(2)}) copy-start(s32[1,256]{1,0:T(1,128)} %param.18) | copy-start | bytes 3076
  7.2 15.8 %copy-start.33 = (s32[1,256]{1,0:T(1,128)S(1)}, s32[1,256]{1,0:T(1,128)}, u32[]{:S(2)}) copy-start(s32[1,256]{1,0:T(1,128)} %param.19) | copy-start | bytes 3076
  7.2 372.2 %all-reduce.4.cloned.1.call-start = ((), (), s32[]{:S(2)}) async-start(), calls=%async_computation | async-start | bytes 25886720
  11.0 29.3 %collective-permute-start.3 = (bf16[16,49,256]{2,0,1:T(8,128)(2,1)}, bf16[16,49,256]{2,0,1:T(8,128)(2,1)}, u32[]{:S(2)}, u32[]{:S(2)}) collective-permute-start(bf16[16,49,256]{2,0,1:T(8,128)(2,1)} %pad_maximum_fusion.1), channel_id=1, source_target_pairs={{8,0},{12,4},{16,8},{20,12},{24,16},{28,20},{32,24},{36,28},{40,32... | collective-permute-start | bytes 1204232 | tf_op jit(solution)/shard_map/ppermute | solution.py:19
  19.1 20.1 %collective-permute-start.2 = (bf16[16,49,256]{2,0,1:T(8,128)(2,1)}, bf16[16,49,256]{2,0,1:T(8,128)(2,1)}, u32[]{:S(2)}, u32[]{:S(2)}) collective-permute-start(bf16[16,49,256]{2,0,1:T(8,128)(2,1)} %pad_maximum_fusion.1), channel_id=1, source_target_pairs={{4,0},{8,4},{12,8},{16,12},{20,16},{24,20},{28,24},{32,28},{36,32}... | collective-permute-start | bytes 1204232 | tf_op jit(solution)/shard_map/ppermute | solution.py:19
  19.2 18.7 %collective-permute-start.1 = (bf16[16,49,256]{2,0,1:T(8,128)(2,1)}, bf16[16,49,256]{2,0,1:T(8,128)(2,1)}, u32[]{:S(2)}, u32[]{:S(2)}) collective-permute-start(bf16[16,49,256]{2,0,1:T(8,128)(2,1)} %pad_maximum_fusion.1), channel_id=1, source_target_pairs={{252,0},{0,4},{4,8},{8,12},{12,16},{16,20},{20,24},{24,28},{28,32}... | collective-permute-start | bytes 1204232 | tf_op jit(solution)/shard_map/ppermute | solution.py:19
  19.6 17.3 %collective-permute-start = (bf16[16,49,256]{2,0,1:T(8,128)(2,1)}, bf16[16,49,256]{2,0,1:T(8,128)(2,1)}, u32[]{:S(2)}, u32[]{:S(2)}) collective-permute-start(bf16[16,49,256]{2,0,1:T(8,128)(2,1)} %pad_maximum_fusion.1), channel_id=1, source_target_pairs={{248,0},{252,4},{0,8},{4,12},{8,16},{12,20},{16,24},{20,28},{24,32... | collective-permute-start | bytes 1204232 | tf_op jit(solution)/shard_map/ppermute | solution.py:19
  20.3 36.7 %copy-start.34 = (bf16[256]{0:T(256)(128)(2,1)}, bf16[256]{0:T(256)(128)(2,1)S(1)}, u32[]{:S(2)}) copy-start(bf16[256]{0:T(256)(128)(2,1)S(1)} %slice_reduce_fusion.1) | copy-start | bytes 1540
  20.4 13.0 %copy-start.23 = (bf16[256,11]{0,1:T(8,128)(2,1)}, bf16[256,11]{0,1:T(8,128)(2,1)S(1)}, u32[]{:S(2)}) copy-start(bf16[256,11]{0,1:T(8,128)(2,1)S(1)} %slice_bitcast_fusion.29) | copy-start | bytes 16900
  23.0 34.0 %copy-start.28 = (pred[256]{0:T(512)(128)(4,1)}, pred[256]{0:T(512)(128)(4,1)S(1)}, u32[]{:S(2)}) copy-start(pred[256]{0:T(512)(128)(4,1)S(1)} %iota_compare_fusion.5) | copy-start | bytes 772
  23.0 7.5 %copy-start.26 = (s32[1,256]{1,0:T(1,128)}, s32[1,256]{1,0:T(1,128)S(1)}, u32[]{:S(2)}) copy-start(s32[1,256]{1,0:T(1,128)S(1)} %broadcast_subtract_fusion) | copy-start | bytes 3076
  23.7 8.0 %copy-start.17 = (bf16[256,16,5]{0,2,1:T(8,128)(2,1)}, bf16[256,16,5]{0,2,1:T(8,128)(2,1)S(1)}, u32[]{:S(2)}) copy-start(bf16[256,16,5]{0,2,1:T(8,128)(2,1)S(1)} %broadcast_multiply_fusion.11) | copy-start | bytes 122884
  23.9 2.9 copy-start.7
  23.9 8.1 %copy-start.15 = (bf16[256,16,7]{0,2,1:T(8,128)(2,1)}, bf16[256,16,7]{0,2,1:T(8,128)(2,1)S(1)}, u32[]{:S(2)}) copy-start(bf16[256,16,7]{0,2,1:T(8,128)(2,1)S(1)} %broadcast_multiply_fusion.10) | copy-start | bytes 172036
  24.0 2.8 copy-start.9
  35.6 1.3 copy-start.3
  37.9 6.3 %slice-start = ((s8[6422528]{0:T(1024)(128)(4,1)}), s8[4194304]{0:T(1024)(128)(4,1)S(1)}, s32[]{:S(2)}) async-start(s8[6422528]{0:T(1024)(128)(4,1)} %bitcast.265), calls=%async_computation.1 | async-start | bytes 8388608
  41.4 1.0 copy-start.8
  41.4 1.3 copy-start.10
  41.4 2.8 slice-start.1
  47.3 7.7 %slice-start.2 = ((s8[6422528]{0:T(1024)(128)(4,1)}), s8[2228224]{0:T(1024)(128)(4,1)S(1)}, s32[]{:S(2)}) async-start(s8[6422528]{0:T(1024)(128)(4,1)} %bitcast.267), calls=%async_computation.3 | async-start | bytes 4456448
  51.2 3.8 slice-start.3
  55.0 2.1 copy-start.22
  55.0 2.4 copy-start.20
  55.1 2.6 copy-start.19
  57.0 1.1 copy-start.14
  57.0 1.4 copy-start.13
  57.2 1.5 copy-start.12
  60.2 29.9 %collective-permute-start.4 = (bf16[16,49,256]{2,0,1:T(8,128)(2,1)}, bf16[16,49,256]{2,0,1:T(8,128)(2,1)}, u32[]{:S(2)}, u32[]{:S(2)}) collective-permute-start(bf16[16,49,256]{2,0,1:T(8,128)(2,1)} %get-tuple-element.9), channel_id=1, source_target_pairs={{8,0},{12,4},{16,8},{20,12},{24,16},{28,20},{32,24},{36,28},{40,32... | collective-permute-start | bytes 1204232 | tf_op jit(solution)/shard_map/ppermute | solution.py:19
  64.9 25.2 %collective-permute-start.7 = (bf16[16,49,256]{2,0,1:T(8,128)(2,1)}, bf16[16,49,256]{2,0,1:T(8,128)(2,1)}, u32[]{:S(2)}, u32[]{:S(2)}) collective-permute-start(bf16[16,49,256]{2,0,1:T(8,128)(2,1)} %get-tuple-element.10), channel_id=1, source_target_pairs={{248,0},{252,4},{0,8},{4,12},{8,16},{12,20},{16,24},{20,28},{24,32... | collective-permute-start | bytes 1204232 | tf_op jit(solution)/shard_map/ppermute | solution.py:19
  64.9 25.2 %collective-permute-start.6 = (bf16[16,49,256]{2,0,1:T(8,128)(2,1)}, bf16[16,49,256]{2,0,1:T(8,128)(2,1)}, u32[]{:S(2)}, u32[]{:S(2)}) collective-permute-start(bf16[16,49,256]{2,0,1:T(8,128)(2,1)} %get-tuple-element.11), channel_id=1, source_target_pairs={{252,0},{0,4},{4,8},{8,12},{12,16},{16,20},{20,24},{24,28},{28,32}... | collective-permute-start | bytes 1204232 | tf_op jit(solution)/shard_map/ppermute | solution.py:19
  65.1 25.0 %collective-permute-start.5 = (bf16[16,49,256]{2,0,1:T(8,128)(2,1)}, bf16[16,49,256]{2,0,1:T(8,128)(2,1)}, u32[]{:S(2)}, u32[]{:S(2)}) collective-permute-start(bf16[16,49,256]{2,0,1:T(8,128)(2,1)} %get-tuple-element.12), channel_id=1, source_target_pairs={{4,0},{8,4},{12,8},{16,12},{20,16},{24,20},{28,24},{32,28},{36,32}... | collective-permute-start | bytes 1204232 | tf_op jit(solution)/shard_map/ppermute | solution.py:19
  76.5 13.6 %copy-start.5 = (bf16[1,16,49,256]{3,1,2,0:T(8,128)(2,1)S(1)}, bf16[1,16,49,256]{3,1,2,0:T(8,128)(2,1)}, u32[]{:S(2)}) copy-start(bf16[1,16,49,256]{3,1,2,0:T(8,128)(2,1)} %param.21) | copy-start | bytes 1204228
  90.1 3.4 copy-start.31
  92.6 0.9 copy-start.11
  94.4 0.8 copy-start.21
  94.4 0.9 copy-start.16
  94.4 0.9 copy-start.18
  94.4 1.0 copy-start.24
  97.2 2.9 copy-start.2
  100.2 2.2 copy-start.27
  100.2 2.2 copy-start.29
  100.2 2.2 copy-start.35
  102.4 1.2 copy-start.6
  102.4 280.1 %copy-start.1 = (f32[90,256]{1,0:T(8,128)S(1)}, f32[90,256]{1,0:T(8,128)}, u32[]{:S(2)}) copy-start(f32[90,256]{1,0:T(8,128)} %param.14) | copy-start | bytes 276484
Sparse Core Ops, SparseCore 0:
  94.6 284.8 all-reduce.3
where the time goes:
time: 390 us; the launch traced here: 389 us
  waiting for transfers between devices  201 us (52%)
  blocking collectives  72.7 us (19%)
  local copies, waits for them, and re-layouts  42 us (11%)
  matrix products  23.6 us (6%)
  starting transfers between devices  19 us (5%)
  between operations  16.5 us (4%)
  other arithmetic  14.1 us (4%)
    unnamed x2, waiting for transfers between devices  201 us
    psum x1, blocking collectives, local(): lax.psum((species_part, charge_part), ('graph', 'rep'))  72.7 us
    ppermute x8, starting transfers between devices, from_behind(): return lax.ppermute(block, axis, route)  19 us
    reshape x1, local copies, waits for them, and re-layouts, local(): flat_grad = weight_part.reshape(-1)  13.6 us
    unnamed x85, local copies, waits for them, and re-layouts  10.1 us
    dot_general x15, matrix products, contract_rows(): lax.dot_general(left_mat, right_mat, (((0,), (0,)), ((), ())), preferred_...  9.34 us
  transfers between devices with their start and end apart: 9, of which 1 were waited for; matrix products, arithmetic and copies ran while one was open for 12% of the time, Pallas kernels for 0%

commit v1 on v0

v1 whole, which is shorter than its diff:
```python
import jax
import jax.numpy as jnp
from jax import lax
from jax.experimental import pallas as pl
from jax.experimental.pallas import tpu as pltpu
from jax.sharding import Mesh
from jax.sharding import PartitionSpec as P


LMAX = 6
DEGREES = LMAX + 1
COEF = DEGREES * DEGREES
CH = 256
FEAT = DEGREES * CH
SPECIES = 90
CHARGES = 9
REACH = 2
BLOCKS = 2 * REACH + 1
HERE = 16
ROWS = COEF * HERE
SLOTS = 256
LIVE = 192
GRAPH = 64
NX, NZ, NC, NY = 4, 8, 2, 4
OUT_ROWS = 7
YROWS = NZ * OUT_ROWS
XROWS = NY * YROWS
HALF = FEAT // 2
LEFT = 768
RIGHT = FEAT - LEFT
TABLE = 112
TABLE_ROWS = 24
MSG_SCALE = 0.25
F32, BF16 = jnp.float32, jnp.bfloat16


VMEM = pl.BlockSpec(memory_space=pltpu.VMEM)
SMEM = pl.BlockSpec(memory_space=pltpu.SMEM)
KEPT = pl.BlockSpec(memory_space=pltpu.VMEM)
HBM = pl.BlockSpec(memory_space=pltpu.HBM)


def call(kernel, out_shape, in_specs, scratch=(), flops=0, moved=0, limit=20):
    run = pl.pallas_call(
        kernel,
        out_shape=out_shape,
        in_specs=in_specs,
        out_specs=jax.tree.map(lambda _: VMEM, out_shape),
        scratch_shapes=list(scratch),
        cost_estimate=pl.CostEstimate(flops=flops, bytes_accessed=moved, transcendentals=0),
        compiler_params=pltpu.CompilerParams(vmem_limit_bytes=limit << 20),
    )

    def placed(*args):
        kept = [
            arg if spec is SMEM else pltpu.with_memory_space_constraint(arg, pltpu.VMEM if spec is KEPT else pltpu.HBM)
            for spec, arg in zip(in_specs, args, strict=True)
        ]
        return run(*kept)

    return placed


def shaped(shape, dtype):
    return jax.ShapeDtypeStruct(shape, dtype)


def matmul(left, right):
    return jnp.dot(left, right, preferred_element_type=F32)


def matmul_nt(left, right):
    return lax.dot_general(left, right, (((1,), (1,)), ((), ())), preferred_element_type=F32)


def span(degree):
    return degree * degree, 2 * degree + 1


def as_column(row):
    wide = jnp.broadcast_to(row.astype(F32), (8, SLOTS))
    return jnp.transpose(wide)[:LIVE, :1]


def lane_ids(width):
    return lax.broadcasted_iota(jnp.int32, (1, width), 1)


def spread_frame(frame_t, degree):
    first, count = span(degree)
    width = HERE * count
    coef = lax.broadcasted_iota(jnp.int32, (COEF, width), 0)
    lane = lax.broadcasted_iota(jnp.int32, (COEF, width), 1)
    pick = jnp.where(coef - first == lane // HERE, 1.0, 0.0).astype(BF16)
    return matmul(frame_t, pick)


def frame_transposed(frame_ref):
    return jnp.transpose(frame_ref[...].astype(F32))[:LIVE].astype(BF16)


def live_row(count_ref):
    return lax.broadcasted_iota(jnp.int32, (1, SLOTS), 1) < count_ref[0, 0]


def target_row(dst_ref, live):
    return jnp.where(live, dst_ref[...] & (HERE - 1), -1)


def source_row(src_ref, dst_ref, live):
    block = (src_ref[...] // HERE - dst_ref[...] // HERE + REACH) & (GRAPH - 1)
    return jnp.where(live, block * HERE + (src_ref[...] & (HERE - 1)), -1)


def embed_kernel(species_ref, charge_ref, feats_ref, table_ref, charge_table_ref, out_ref, emb, ids, head, sems):
    rest = pltpu.make_async_copy(feats_ref.at[HERE:ROWS], out_ref.at[HERE:ROWS], sems.at[0])
    rest.start()
    first = pltpu.make_async_copy(feats_ref.at[0:HERE], head, sems.at[1])
    first.start()
    for atom in range(HERE):
        kind = species_ref[0, atom]
        emb[atom : atom + 1, :] = table_ref[pl.ds(kind, 1), :] + charge_table_ref[pl.ds(charge_ref[0], 1), :]
        ids[atom : atom + 1, :] = jnp.full((1, CH), kind, jnp.int32)
    out_ref[ROWS : ROWS + HERE] = ids[...].astype(F32).astype(BF16)
    first.wait()
    out_ref[0:HERE] = (head[...].astype(F32) + emb[...]).astype(BF16)
    rest.wait()


def cotangent_kernel(count_ref, dst_ref, frame_ref, cot_ref, out_ref):
    target = as_column(target_row(dst_ref, live_row(count_ref)))
    frame_t = frame_transposed(frame_ref)
    for degree in range(DEGREES):
        first, count = span(degree)
        width = HERE * count
        atom = (lane_ids(width) & (HERE - 1)).astype(F32)
        coefs = jnp.where(target == atom, spread_frame(frame_t, degree), 0.0).astype(BF16)
        grads = matmul(coefs, cot_ref[first * HERE : first * HERE + width])
        out_ref[:, degree * CH : (degree + 1) * CH] = MSG_SCALE * grads


def source_coefs(source_slots, frame, first, count, indices=range(BLOCKS)):
    atom = lax.broadcasted_iota(jnp.int32, (HERE, SLOTS), 0)
    pieces = []
    for index in indices:
        mask = source_slots - HERE * index == atom
        for k in range(first, first + count):
            row = jnp.broadcast_to(frame[k : k + 1, :], (HERE, SLOTS))
            pieces.append(jnp.where(mask, row, 0.0).astype(BF16))
    return jnp.concatenate(pieces, axis=0)[:, :LIVE]


def edge_kernel(
    count_ref, core_ref, charge_ref, src_ref, dst_ref, frame_ref, behind_ref, own_ref, ahead_ref, partner_ref,
    passed_ref, weight_hbm, grad_values_ref, row_ids_ref, rot, theirs_ref, values_ref,
    grad_pre_ref, grad_pre_t_ref, table_mine_ref, table_theirs_ref, weight, sems, pre_ref, stage,
):
    copies = []
    for degree in range(DEGREES):
        cols = pl.ds(degree * CH, CH)
        copies.append(pltpu.make_async_copy(weight_hbm.at[:, cols], weight.at[:, cols], sems.at[degree]))
        copies[-1].start()
    core = core_ref[0]
    blocks = (
        (behind_ref, 0),
        (own_ref, REACH),
        (ahead_ref, 2 * REACH),
        (partner_ref, REACH + 1 - 2 * core),
        (passed_ref, REACH - 1 + 2 * core),
    )
    source_slots = source_row(src_ref, dst_ref, live_row(count_ref))
    source = as_column(source_slots)
    frame_t = frame_transposed(frame_ref)
    for degree in range(DEGREES):
        first, count = span(degree)
        width = HERE * count
        atom = (lane_ids(width) & (HERE - 1)).astype(F32)
        frame_cols = spread_frame(frame_t, degree)
        total = jnp.zeros((LIVE, CH), F32)
        for block, index in blocks:
            wanted = atom + jnp.asarray(HERE * index, jnp.int32).astype(F32)
            coefs = jnp.where(source == wanted, frame_cols, 0.0).astype(BF16)
            total = total + matmul(coefs, block[first * HERE : first * HERE + width])
        rot[:, degree * CH : (degree + 1) * CH] = total.astype(BF16)
    permute_rows(row_ids_ref, 1 - core, rot, theirs_ref)
    for copy in copies:
        copy.wait()
    pre_ref[...] = matmul(rot[...], weight[...])
    gate = jax.nn.sigmoid(pre_ref[:, 0:CH])
    cross = None
    for degree in range(DEGREES):
        cols = slice(degree * CH, (degree + 1) * CH)
        pre = pre_ref[:, cols]
        values_ref[:, cols] = (pre * gate).astype(BF16)
        grads = grad_values_ref[:, cols]
        cross = grads * pre if degree == 0 else cross + grads * pre
        if degree:
            grad_pre_ref[:, cols] = (grads * gate).astype(BF16)
    head = grad_values_ref[:, 0:CH] * gate + cross * gate * (1.0 - gate)
    grad_pre_ref[:, 0:CH] = head.astype(BF16)
    grad_pre_t = jnp.transpose(grad_pre_ref[...])
    grad_pre_t_ref[...] = grad_pre_t
    work_t = matmul(weight[0:CH, :], grad_pre_t).astype(BF16)
    terms = matmul_nt(source_coefs(source_slots, frame_ref[0:1, :].astype(F32), 0, 1, [i for _, i in blocks]), work_t)
    terms = terms.astype(BF16)
    kinds = lax.broadcasted_iota(jnp.int32, (HERE, 128), 1)
    hots = []
    for block, _ in blocks:
        own = block[ROWS : ROWS + HERE, 0:128].astype(F32).astype(jnp.int32)
        hot = (kinds == own) | (kinds == SPECIES + charge_ref[0])
        hots.append(jnp.where(hot, 1.0, 0.0).astype(BF16))
    hot = jnp.concatenate(hots, axis=0)
    table = lax.dot_general(hot, terms, (((0,), (0,)), ((), ())), preferred_element_type=F32)
    stage[...] = table[:TABLE]
    half = TABLE // 2
    table_mine_ref[...] = stage[pl.ds(pl.multiple_of(core * half, 8), half), :]
    table_theirs_ref[...] = stage[pl.ds(pl.multiple_of((1 - core) * half, 8), half), :]


def source_kernel(
    count_ref, src_ref, dst_ref, frame_ref, grad_pre_t_ref, weight_hbm, o0, o1, o2, o3, o4, weight, sems
):
    copies = []
    for degree in range(DEGREES):
        rows = pl.ds(degree * CH, CH)
        copies.append(pltpu.make_async_copy(weight_hbm.at[rows], weight.at[rows], sems.at[degree]))
        copies[-1].start()
    outs = (o0, o1, o2, o3, o4)
    source_slots = source_row(src_ref, dst_ref, live_row(count_ref))
    frame = frame_ref[...].astype(F32)
    for degree in range(DEGREES):
        first, count = span(degree)
        width = HERE * count
        copies[degree].wait()
        work_t = matmul(weight[degree * CH : (degree + 1) * CH, :], grad_pre_t_ref[...]).astype(BF16)
        terms = matmul_nt(source_coefs(source_slots, frame, first, count), work_t).astype(BF16)
        for index, out_ref in enumerate(outs):
            out_ref[first * HERE : first * HERE + width] = terms[index * width : (index + 1) * width]


def target_kernel(count_ref, dst_ref, frame_ref, values_ref, feats_ref, out_ref):
    target = target_row(dst_ref, live_row(count_ref))
    mask = target == lax.broadcasted_iota(jnp.int32, (HERE, SLOTS), 0)
    frame = frame_ref[...].astype(F32)
    for degree in range(DEGREES):
        first, count = span(degree)
        rows = slice(first * HERE, (first + count) * HERE)
        pieces = [
            jnp.where(mask, jnp.broadcast_to(frame[k : k + 1, :], (HERE, SLOTS)), 0.0).astype(BF16)
            for k in range(first, first + count)
        ]
        coefs = jnp.concatenate(pieces, axis=0)[:, :LIVE]
        total = matmul(coefs, values_ref[:, degree * CH : (degree + 1) * CH])
        out_ref[rows] = (feats_ref[rows].astype(F32) + MSG_SCALE * total).astype(BF16)


def finish_kernel(r0, r1, r2, r3, r4, cot_ref, out_ref):
    @pl.loop(0, COEF)
    def _(k):
        rows = pl.ds(pl.multiple_of(k * HERE, HERE), HERE)
        total = r0[rows].astype(F32)
        for term in (r1, r2, r3, r4):
            total = total + term[rows].astype(F32)
        out_ref[rows] = (cot_ref[rows].astype(F32) + total).astype(BF16)


def fold_table(table, out_ref, start):
    out_ref[start : start + TABLE_ROWS, 0:CH] = table[0:TABLE_ROWS]
    out_ref[start : start + TABLE_ROWS, CH : 2 * CH] = table[TABLE_ROWS : 2 * TABLE_ROWS]
    tail = jnp.concatenate([table[2 * TABLE_ROWS :], jnp.zeros((16, CH), BF16)], axis=0)
    out_ref[start : start + TABLE_ROWS, 2 * CH : 3 * CH] = tail


def permute_rows(row_ids_ref, half, rot, out_ref):
    window = lax.broadcasted_iota(jnp.int32, (XROWS, 512), 1)
    for odd in range(2):
        wanted = row_ids_ref[...] + (64 * odd + NY * OUT_ROWS * half)
        pick = jnp.where(window == wanted, 1.0, 0.0).astype(BF16)
        for pair in range(2):
            start = pair * HALF + 384 * odd
            out_ref[2 * pair + odd] = matmul_nt(pick, rot[:, start : start + 512]).astype(BF16)


def own_rows_kernel(core_ref, row_ids_ref, rot_ref, out_ref):
    permute_rows(row_ids_ref, core_ref[0], rot_ref, out_ref)


def outer_kernel(
    place_ref, mine_ref, gift_ref, grad_ref, gift_grad_ref, table_ref, gift_table_ref, a0, a1, a2, a3,
    c0, c1, c2, c3, stage
):
    outs_x, outs_y = (a0, a1, a2, a3), (c0, c1, c2, c3)
    table = (table_ref[...] + gift_table_ref[...]).astype(BF16)
    for step, out_ref in enumerate(outs_x):
        fold_table(table, out_ref, XROWS)
        block = (place_ref[0] + step) & (NX - 1)
        out_ref[0:XROWS] = (
            matmul(mine_ref[block], grad_ref[:, :LEFT]) + matmul(gift_ref[block], gift_grad_ref[:, :LEFT])
        ).astype(BF16)
    for block in range(NX):
        stage[...] = matmul(mine_ref[block], grad_ref[:, LEFT:]) + matmul(gift_ref[block], gift_grad_ref[:, LEFT:])
        for step, out_ref in enumerate(outs_y):
            first = pl.multiple_of(((place_ref[1] + step) & (NY - 1)) * YROWS, 8)
            out_ref[block] = stage[pl.ds(first, YROWS), :].astype(BF16)


def first_sum_kernel(place_ref, a0, a1, a2, a3, c0, c1, c2, c3, s0, s1, s2, s3, t0, t1, t2, t3, stage):
    stage[...] = sum(r[...].astype(F32) for r in (a1, a2, a3)) + a0[...].astype(F32)
    table = stage[XROWS : XROWS + TABLE_ROWS, :].astype(BF16)
    for step, out_ref in enumerate((s0, s1, s2, s3)):
        first = pl.multiple_of(((place_ref[1] + step) & (NY - 1)) * YROWS, 8)
        out_ref[0:YROWS] = stage[pl.ds(first, YROWS), :].astype(BF16)
        out_ref[YROWS : YROWS + TABLE_ROWS] = table
    for step, out_ref in enumerate((t0, t1, t2, t3)):
        block = (place_ref[0] + step) & (NX - 1)
        out_ref[...] = sum(r[block].astype(F32) for r in (c0, c1, c2, c3)).astype(BF16)


def second_sum_kernel(s0, s1, s2, s3, t0, t1, t2, t3, out_ref):
    left = sum(r[...].astype(F32) for r in (s0, s1, s2, s3))
    right = sum(r[...].astype(F32) for r in (t0, t1, t2, t3))
    for block in range(NZ):
        rows = slice(block * OUT_ROWS, (block + 1) * OUT_ROWS)
        out_ref[block, 8:15, 0:LEFT] = left[rows].astype(BF16)
        out_ref[block, 8:15, LEFT:FEAT] = right[rows].astype(BF16)
        for piece in range(DEGREES):
            first = YROWS + 8 * (piece % 3)
            third = slice(piece // 3 * CH, (piece // 3 + 1) * CH)
            out_ref[block, 0:8, piece * CH : (piece + 1) * CH] = left[first : first + 8, third].astype(BF16)


def close_kernel(last_ref, weight_ref, table_ref):
    total = sum((last_ref[block].astype(F32) for block in range(1, NZ)), last_ref[0].astype(F32))
    weight_ref[...] = total[8:15]
    for piece in range(DEGREES):
        table_ref[8 * piece : 8 * piece + 8] = total[0:8, piece * CH : (piece + 1) * CH]


def join_kernel(core_ref, mine_ref, other_ref, species_ref, charge_ref, stage):
    half = TABLE // 2
    stage[pl.ds(pl.multiple_of(core_ref[0] * half, 8), half), :] = mine_ref[...]
    stage[pl.ds(pl.multiple_of((1 - core_ref[0]) * half, 8), half), :] = other_ref[...]
    species_ref[...] = stage[:SPECIES]
    charge_ref[...] = stage[SPECIES : SPECIES + CHARGES]


def shift(block, axes, size, distance):
    return lax.ppermute(block, axes, [(i, (i + distance) % size) for i in range(size)])


def swap(block, axis, size, mask):
    return lax.ppermute(block, axis, [(i, i ^ mask) for i in range(size)])


def local(
    node_feats, species, charge, species_table, charge_table, so2_weight, edge_frame, edge_src, edge_dst,
    edge_count, out_cotangent,
):
    feats = jnp.transpose(node_feats[0], (1, 0, 2)).reshape(ROWS, CH)
    cotangent = jnp.transpose(out_cotangent[0], (1, 0, 2)).reshape(ROWS, CH)
    frame = edge_frame[0]
    core = lax.axis_index("c").astype(jnp.int32).reshape(1)
    place = jnp.stack([lax.axis_index("x"), lax.axis_index("y")]).astype(jnp.int32)
    ring = ("x", "z", "c")

    hidden = call(
        embed_kernel,
        shaped((ROWS + HERE, CH), BF16),
        [SMEM, SMEM, HBM, VMEM, VMEM],
        [
            pltpu.VMEM((HERE, CH), F32),
            pltpu.VMEM((HERE, CH), jnp.int32),
            pltpu.VMEM((HERE, CH), BF16),
            pltpu.SemaphoreType.DMA((2,)),
        ],
        moved=900000,
    )(species, charge, feats, species_table, charge_table)
    behind = shift(hidden, ring, GRAPH, REACH)
    ahead = shift(hidden, ring, GRAPH, -REACH)
    partner = swap(hidden, "c", NC, 1)
    passed = swap(jnp.where(core[0] == 0, ahead, behind), "c", NC, 1)
    grad_values = call(
        cotangent_kernel, shaped((LIVE, FEAT), F32), [SMEM, VMEM, VMEM, VMEM], flops=2 * LIVE * ROWS * CH, moved=1800000
    )(edge_count, edge_dst, frame, cotangent)
    ids = jnp.arange(XROWS, dtype=jnp.int32)
    row_ids = (ids % YROWS // OUT_ROWS * (NC * NY * OUT_ROWS) + ids // YROWS * OUT_ROWS + ids % OUT_ROWS)[:, None]
    rotated, theirs, values, grad_pre, grad_pre_t, table, table_theirs = call(
        edge_kernel,
        (
            shaped((LIVE, FEAT), BF16),
            shaped((NX, XROWS, LIVE), BF16),
            shaped((LIVE, FEAT), BF16),
            shaped((LIVE, FEAT), BF16),
            shaped((FEAT, LIVE), BF16),
            shaped((TABLE // 2, CH), F32),
            shaped((TABLE // 2, CH), F32),
        ),
        [SMEM, SMEM, SMEM, VMEM, VMEM, VMEM]
        + [KEPT] * BLOCKS
        + [HBM, KEPT, KEPT],
        [
            pltpu.VMEM((FEAT, FEAT), BF16),
            pltpu.SemaphoreType.DMA((DEGREES,)),
            pltpu.VMEM((LIVE, FEAT), F32),
            pltpu.VMEM((TABLE, CH), F32),
        ],
        flops=2 * LIVE * FEAT * FEAT,
        moved=12000000,
    )(edge_count, core, charge, edge_src, edge_dst, frame, behind, hidden, ahead, partner, passed, so2_weight, grad_values, row_ids)
    gift = swap(theirs, "c", NC, 1)
    gift_grad = swap(grad_pre, "c", NC, 1)
    gift_table = swap(table_theirs, "c", NC, 1)
    mine = call(
        own_rows_kernel, shaped((NX, XROWS, LIVE), BF16), [SMEM, KEPT, KEPT], flops=2 * LIVE * HALF * 512, moved=1200000
    )(core, row_ids, rotated)
    terms = call(
        source_kernel,
        (shaped((ROWS, CH), BF16),) * BLOCKS,
        [SMEM, VMEM, VMEM, VMEM, KEPT, HBM],
        [pltpu.VMEM((FEAT, FEAT), BF16), pltpu.SemaphoreType.DMA((DEGREES,))],
        flops=2 * LIVE * FEAT * FEAT,
        moved=9000000,
    )(edge_count, edge_src, edge_dst, frame, grad_pre_t, so2_weight)
    returned = [
        terms[offset + REACH] if offset == 0 else shift(terms[offset + REACH], ring, GRAPH, offset)
        for offset in range(-REACH, REACH + 1)
    ]
    outer = call(
        outer_kernel,
        (shaped((XROWS + TABLE_ROWS, LEFT), BF16),) * NX + (shaped((NX, YROWS, RIGHT), BF16),) * NY,
        [SMEM] + [KEPT] * 6,
        [pltpu.VMEM((XROWS, RIGHT), F32)],
        flops=4 * LIVE * HALF * FEAT,
        moved=6000000,
    )(place, mine, gift, grad_pre, gift_grad, table, gift_table)
    along_x, along_y = list(outer[:NX]), list(outer[NX:])
    for step in (2, 1, 3):
        along_x[step] = shift(along_x[step], "x", NX, step)
        along_y[step] = shift(along_y[step], "y", NY, step)
    updated = call(
        target_kernel,
        shaped((ROWS, CH), BF16),
        [SMEM, VMEM, VMEM, KEPT, VMEM],
        flops=2 * LIVE * ROWS * CH,
        moved=1800000,
    )(edge_count, edge_dst, frame, values, feats)
    feat_grad = call(
        finish_kernel, shaped((ROWS, CH), BF16), [KEPT] * BLOCKS + [VMEM], moved=2800000
    )(*returned, cotangent)
    first = call(
        first_sum_kernel,
        (shaped((YROWS + TABLE_ROWS, LEFT), BF16),) * NX + (shaped((YROWS, RIGHT), BF16),) * NY,
        [SMEM] + [KEPT] * 8,
        [pltpu.VMEM((XROWS + TABLE_ROWS, LEFT), F32)],
        moved=4000000,
    )(place, *along_x, *along_y)
    then_y, then_x = list(first[:NY]), list(first[NY:])
    for step in (2, 1, 3):
        then_y[step] = shift(then_y[step], "y", NY, step)
        then_x[step] = shift(then_x[step], "x", NX, step)
    last = call(second_sum_kernel, shaped((NZ, 15, FEAT), BF16), [KEPT] * 8, moved=1000000)(*then_y, *then_x)
    last = lax.all_to_all(last, "z", 0, 0)
    weight_rows, table = call(
        close_kernel, (shaped((OUT_ROWS, FEAT), F32), shaped((TABLE // 2, CH), F32)), [KEPT], moved=600000
    )(last)
    other = swap(table, "c", NC, 1)
    weight_grad = weight_rows.reshape(-1)
    species_grad, charge_grad = call(
        join_kernel,
        (shaped((SPECIES, CH), F32), shaped((CHARGES, CH), F32)),
        [SMEM, KEPT, KEPT],
        [pltpu.VMEM((TABLE, CH), F32)],
        moved=200000,
    )(core, table, other)

    def restore(rows):
        return jnp.transpose(rows.reshape(COEF, HERE, CH), (1, 0, 2))[None]

    return (
        restore(updated),
        restore(feat_grad),
        weight_grad,
        species_grad,
        charge_grad,
    )


def solution(mesh):
    fine = Mesh(mesh.devices.reshape(NX, NZ, NC, NY), ("x", "z", "c", "y"))
    graph = ("x", "z", "c")
    in_specs = (
        P("y", graph, None, None),
        P("y", graph),
        P("y"),
        P(),
        P(),
        P(),
        P("y", None, graph),
        P("y", graph),
        P("y", graph),
        P("y", graph),
        P("y", graph, None, None),
    )
    out_specs = (
        P("y", graph, None, None),
        P("y", graph, None, None),
        P(("x", "z", "c", "y")),
        P(),
        P(),
    )
    return jax.shard_map(local, mesh=fine, in_specs=in_specs, out_specs=out_specs, check_vma=False)
```

time: 390 us -> 133 us (0.34)
  the two profiles are of different devices: /device:TPU:8 before, /device:TPU:1 now
where the time goes in v1:
time: 133 us
  waiting for transfers between devices  56.9 us (43%)
  starting transfers between devices  38.6 us (29%)
  Pallas kernels  31.5 us (24%)
  local copies, waits for them, and re-layouts  3.24 us (2%)
  between operations  2.09 us (2%)
    ppermute x18, waiting for transfers between devices, shift(): lax.ppermute(block, axes, [(i, (i + distance) % size) for i in range(size)])  56 us
    pallas_call x12, Pallas kernels, placed(): return run(*kept)  31.5 us
    ppermute x18, starting transfers between devices, shift(): lax.ppermute(block, axes, [(i, (i + distance) % size) for i in range(size)])  31.2 us
    ppermute x6, starting transfers between devices, swap(): return lax.ppermute(block, axis, [(i, i ^ mask) for i in range(size)])  3.96 us
    all_to_all x1, starting transfers between devices, local(): last = lax.all_to_all(last, 'z', 0, 0)  3.47 us
  transfers between devices with their start and end apart: 25, of which 10 were waited for; matrix products, arithmetic and copies ran while one was open for 1% of the time, Pallas kernels for 12%

profile of v1, /device:TPU:1, one launch (start us, length us, event | category | flops | bytes accessed | tf_op | source)
XLA Modules:
  0.0 132.7 jit_solution(12746504253075399312)
XLA Ops:
  1.3 0.6 copy-done.2
  1.9 1.9 %shard_map.146.own_ref = bf16[800,256]{1,0:T(8,128)(2,1)S(1)} custom-call(s32[1,16]{1,0:T(1,128)S(1)} %copy-done.2, s32[1]{0:T(128)S(6)} %copy.16.charge_ref, bf16[784,256]{1,0:T(8,128)(2,1)} %bitcast.24, f32[90,256]{1,0:T(8,128)} %table_ref.1, f32[9,256]{1,0:T(8,128)} %charge_table_ref.1), custom_call_target="tpu_custom_call" | custom-call | bytes 900000 | tf_op jit(solution)/shard_map/pallas_call | solution.py:59
  3.9 8.7 %collective-permute-start.1 = (bf16[800,256]{1,0:T(8,128)(2,1)S(1)}, bf16[800,256]{1,0:T(8,128)(2,1)S(1)}, u32[]{:S(2)}, u32[]{:S(2)}) collective-permute-start(bf16[800,256]{1,0:T(8,128)(2,1)S(1)} %shard_map.146.own_ref), channel_id=1, source_target_pairs={{0,248},{4,252},{8,0},{12,4},{16,8},{20,12},{24,16},{28,20},{32,24... | collective-permute-start | bytes 1228808 | tf_op jit(solution)/shard_map/ppermute | solution.py:348
  12.5 0.0 collective-permute-start
  12.5 1.0 collective-permute-start.2
  13.5 7.2 %collective-permute-done.1.ahead_ref = bf16[800,256]{1,0:T(8,128)(2,1)S(1)} collective-permute-done((bf16[800,256]{1,0:T(8,128)(2,1)S(1)}, bf16[800,256]{1,0:T(8,128)(2,1)S(1)}, u32[]{:S(2)}, u32[]{:S(2)}) %collective-permute-start.1) | collective-permute-done | bytes 409632 | tf_op jit(solution)/shard_map/ppermute | solution.py:348
  20.7 5.2 %collective-permute-done.behind_ref = bf16[800,256]{1,0:T(8,128)(2,1)S(1)} collective-permute-done((bf16[800,256]{1,0:T(8,128)(2,1)S(1)}, bf16[800,256]{1,0:T(8,128)(2,1)S(1)}, u32[]{:S(2)}, u32[]{:S(2)}) %collective-permute-start) | collective-permute-done | bytes 409632 | tf_op jit(solution)/shard_map/ppermute | solution.py:348
  26.0 1.9 %collective-permute-start.3 = (bf16[800,256]{1,0:T(8,128)(2,1)S(1)}, bf16[800,256]{1,0:T(8,128)(2,1)S(1)}, u32[]{:S(2)}, u32[]{:S(2)}) collective-permute-start(bf16[800,256]{1,0:T(8,128)(2,1)S(1)} %broadcast_select_fusion), channel_id=1, source_target_pairs={{0,4},{4,0},{1,5},{5,1},{2,6},{6,2},{3,7},{7,3},{8,12},{12,8},{9,1... | collective-permute-start | bytes 1228808 | tf_op jit(solution)/shard_map/ppermute | solution.py:352
  28.5 1.9 %shard_map.147.grad_values_ref = f32[192,1792]{1,0:T(8,128)S(1)} custom-call(s32[1,1]{1,0:T(1,128)S(6)} %copy.17.count_ref, s32[1,256]{1,0:T(1,128)} %dst_ref.7, bf16[49,256]{1,0:T(8,128)(2,1)} %bitcast.28, bf16[784,256]{1,0:T(8,128)(2,1)} %bitcast.26), custom_call_target="tpu_custom_call" | custom-call | flops 77070336 | bytes 1800000 | tf_op jit(solution)/shard_map/pallas_call | solution.py:59
  30.4 0.2 fusion.12.row_ids_ref
  30.6 0.0 collective-permute-done.2.partner_ref
  30.6 0.0 collective-permute-done.3.passed_ref
  30.6 7.6 %shard_map.148 = (bf16[192,1792]{1,0:T(8,128)(2,1)S(1)}, bf16[4,224,192]{2,1,0:T(8,128)(2,1)}, bf16[192,1792]{1,0:T(8,128)(2,1)S(1)}, bf16[192,1792]{1,0:T(8,128...) custom-call(s32[1,1]{1,0:T(1,128)S(6)} %copy.17.count_ref, ...), custom_call_target="tpu_custom_call" | custom-call | flops 1233125376 | bytes 12000000 | tf_op jit(solution)/shard_map/pallas_call | solution.py:59
  38.2 0.9 copy-done
  39.1 0.0 collective-permute-start.9
  39.1 0.5 collective-permute-start.8
  39.6 0.0 collective-permute-start.10
  39.6 0.1 pad_add_fusion.place_ref
  39.6 1.1 copy-done.1
  40.7 0.5 shard_map.152.mine_ref
  41.2 0.9 collective-permute-done.10.gift_table_ref
  42.1 0.0 collective-permute-done.8.gift_ref
  42.1 0.0 collective-permute-done.9.gift_grad_ref
  42.2 3.3 %shard_map.153 = (bf16[248,768]{1,0:T(8,128)(2,1)S(1)}, bf16[248,768]{1,0:T(8,128)(2,1)S(1)}, bf16[248,768]{1,0:T(8,128)(2,1)S(1)}, bf16[248,768]{1,0:T(8,128)(2...) custom-call(s32[2]{0:T(128)S(1)} %pad_add_fusion.place_ref, ...), custom_call_target="tpu_custom_call" | custom-call | flops 1233125376 | bytes 6000000 | tf_op jit(solution)/shard_map/pallas_call | solution.py:59
  45.5 0.1 collective-permute-start.11
  45.6 1.6 %collective-permute-start.14 = (bf16[4,56,1024]{2,1,0:T(8,128)(2,1)S(1)}, bf16[4,56,1024]{2,1,0:T(8,128)(2,1)S(1)}, u32[]{:S(2)}, u32[]{:S(2)}) collective-permute-start(bf16[4,56,1024]{2,1,0:T(8,128)(2,1)S(1)} %get-tuple-element.54), channel_id=1, source_target_pairs={{0,1},{1,2},{2,3},{3,0},{4,5},{5,6},{6,7},{7,4},{8,9},{9,10},{10,1... | collective-permute-start | bytes 1376264 | tf_op jit(solution)/shard_map/ppermute | solution.py:348
  47.1 2.6 %collective-permute-start.15 = (bf16[4,56,1024]{2,1,0:T(8,128)(2,1)S(1)}, bf16[4,56,1024]{2,1,0:T(8,128)(2,1)S(1)}, u32[]{:S(2)}, u32[]{:S(2)}) collective-permute-start(bf16[4,56,1024]{2,1,0:T(8,128)(2,1)S(1)} %get-tuple-element.55), channel_id=1, source_target_pairs={{0,2},{1,3},{2,0},{3,1},{4,6},{5,7},{6,4},{7,5},{8,10},{9,11},{10,... | collective-permute-start | bytes 1376264 | tf_op jit(solution)/shard_map/ppermute | solution.py:348
  49.8 1.1 collective-permute-start.16
  50.8 0.3 collective-permute-start.12
  51.1 14.1 %collective-permute-done.11.a1 = bf16[248,768]{1,0:T(8,128)(2,1)S(1)} collective-permute-done((bf16[248,768]{1,0:T(8,128)(2,1)S(1)}, bf16[248,768]{1,0:T(8,128)(2,1)S(1)}, u32[]{:S(2)}, u32[]{:S(2)}) %collective-permute-start.11) | collective-permute-done | bytes 380960 | tf_op jit(solution)/shard_map/ppermute | solution.py:348
  65.2 0.0 collective-permute-start.13
  65.2 0.0 collective-permute-done.12.a2
  65.2 9.4 %collective-permute-done.13.a3 = bf16[248,768]{1,0:T(8,128)(2,1)S(1)} collective-permute-done((bf16[248,768]{1,0:T(8,128)(2,1)S(1)}, bf16[248,768]{1,0:T(8,128)(2,1)S(1)}, u32[]{:S(2)}, u32[]{:S(2)}) %collective-permute-start.13) | collective-permute-done | bytes 380960 | tf_op jit(solution)/shard_map/ppermute | solution.py:348
  74.6 0.0 collective-permute-done.14.c1
  74.6 0.0 collective-permute-done.15.c2
  74.6 0.0 collective-permute-done.16.c3
  74.6 1.2 shard_map.154
  75.9 0.1 collective-permute-start.20
  76.0 1.4 %collective-permute-start.17 = (bf16[80,768]{1,0:T(8,128)(2,1)S(1)}, bf16[80,768]{1,0:T(8,128)(2,1)S(1)}, u32[]{:S(2)}, u32[]{:S(2)}) collective-permute-start(bf16[80,768]{1,0:T(8,128)(2,1)S(1)} %get-tuple-element.58), channel_id=1, source_target_pairs={{0,1},{1,2},{2,3},{3,0},{4,5},{5,6},{6,7},{7,4},{8,9},{9,10},{10,1... | collective-permute-start | bytes 368648 | tf_op jit(solution)/shard_map/ppermute | solution.py:348
  77.3 2.6 %collective-permute-start.18 = (bf16[80,768]{1,0:T(8,128)(2,1)S(1)}, bf16[80,768]{1,0:T(8,128)(2,1)S(1)}, u32[]{:S(2)}, u32[]{:S(2)}) collective-permute-start(bf16[80,768]{1,0:T(8,128)(2,1)S(1)} %get-tuple-element.59), channel_id=1, source_target_pairs={{0,2},{1,3},{2,0},{3,1},{4,6},{5,7},{6,4},{7,5},{8,10},{9,11},{10,... | collective-permute-start | bytes 368648 | tf_op jit(solution)/shard_map/ppermute | solution.py:348
  80.0 1.1 collective-permute-start.19
  81.0 2.6 %collective-permute-start.21 = (bf16[56,1024]{1,0:T(8,128)(2,1)S(1)}, bf16[56,1024]{1,0:T(8,128)(2,1)S(1)}, u32[]{:S(2)}, u32[]{:S(2)}) collective-permute-start(bf16[56,1024]{1,0:T(8,128)(2,1)S(1)} %get-tuple-element.63), channel_id=1, source_target_pairs={{0,128},{64,192},{128,0},{192,64},{1,129},{65,193},{129,1},{193,65... | collective-permute-start | bytes 344072 | tf_op jit(solution)/shard_map/ppermute | solution.py:348
  83.6 0.0 collective-permute-done.20.t1
  83.6 0.0 collective-permute-start.22
  83.6 2.8 %collective-permute-done.21.t2 = bf16[56,1024]{1,0:T(8,128)(2,1)S(1)} collective-permute-done((bf16[56,1024]{1,0:T(8,128)(2,1)S(1)}, bf16[56,1024]{1,0:T(8,128)(2,1)S(1)}, u32[]{:S(2)}, u32[]{:S(2)}) %collective-permute-start.21) | collective-permute-done | bytes 114720 | tf_op jit(solution)/shard_map/ppermute | solution.py:348
  86.5 1.2 collective-permute-done.22.t3
  87.7 0.0 collective-permute-done.17.s1
  87.7 0.0 collective-permute-done.18.s2
  87.7 0.0 collective-permute-done.19.s3
  87.7 1.0 shard_map.155
  88.6 3.5 %all-to-all-start = ((bf16[8,15,1792]{2,1,0:T(8,128)(2,1)}), bf16[8,15,1792]{2,1,0:T(8,128)(2,1)S(1)}, u32[]{:S(2)}, u32[]{:S(2)}) async-start(bf16[8,15,1792]{2,1,0:T(8,128)(2,1)} %shard_map.155), calls=%async_computation | async-start | bytes 917504 | tf_op jit(solution)/shard_map/all_to_all | solution.py:462
  92.1 9.1 %shard_map.150 = (bf16[784,256]{1,0:T(8,128)(2,1)}, bf16[784,256]{1,0:T(8,128)(2,1)}, bf16[784,256]{1,0:T(8,128)(2,1)S(1)}, bf16[784,256]{1,0:T(8,128)(2,1)}, bf16[784,256]{1,0:T(8,128)(2,1)}) custom-call(s32[1,1]{1,0:T(1,128)S(6)} %copy.17.count_ref, s32[1,256]{1,0:T(1,128)} %src_ref.3, s32[1,256]{1,0:T(1,128)} %dst_ref.7, bf16[49,256]{1,0:T(8,128)(2,1)} %bitcast.30, ...), custom_call_target="tpu_custom_call" | custom-call | flops 1233125376 | bytes 9000000 | tf_op jit(solution)/shard_map/pallas_call | solution.py:59
  101.2 4.5 %collective-permute-start.4 = (bf16[784,256]{1,0:T(8,128)(2,1)}, bf16[784,256]{1,0:T(8,128)(2,1)S(1)}, u32[]{:S(2)}, u32[]{:S(2)}) collective-permute-start(bf16[784,256]{1,0:T(8,128)(2,1)} %get-tuple-element.39), channel_id=1, source_target_pairs={{0,248},{4,252},{8,0},{12,4},{16,8},{20,12},{24,16},{28,20},{32,24... | collective-permute-start | bytes 1204232 | tf_op jit(solution)/shard_map/ppermute | solution.py:348
  105.7 4.7 %collective-permute-start.5 = (bf16[784,256]{1,0:T(8,128)(2,1)}, bf16[784,256]{1,0:T(8,128)(2,1)S(1)}, u32[]{:S(2)}, u32[]{:S(2)}) collective-permute-start(bf16[784,256]{1,0:T(8,128)(2,1)} %get-tuple-element.40), channel_id=1, source_target_pairs={{0,252},{4,0},{8,4},{12,8},{16,12},{20,16},{24,20},{28,24},{32,28}... | collective-permute-start | bytes 1204232 | tf_op jit(solution)/shard_map/ppermute | solution.py:348
  110.3 0.0 collective-permute-start.6
  110.4 0.1 shard_map.156
  110.4 0.6 collective-permute-start.23
  111.0 2.1 %shard_map.149 = bf16[784,256]{1,0:T(8,128)(2,1)} custom-call(s32[1,1]{1,0:T(1,128)S(6)} %copy.17.count_ref, s32[1,256]{1,0:T(1,128)} %dst_ref.7, bf16[49,256]{1,0:T(8,128)(2,1)} %bitcast.31, bf16[192,1792]{1,0:T(8,128)(2,1)S(1)} %get-tuple-element.37.values_ref, bf16[784,256]{1,0:T(8,128)(2,1)} %bitcast.25), custom_call_target="tpu_custom_call" | custom-call | flops 77070336 | bytes 1800000 | tf_op jit(solution)/shard_map/pallas_call | solution.py:59
  113.1 5.1 %collective-permute-done.5.r1 = bf16[784,256]{1,0:T(8,128)(2,1)S(1)} collective-permute-done((bf16[784,256]{1,0:T(8,128)(2,1)}, bf16[784,256]{1,0:T(8,128)(2,1)S(1)}, u32[]{:S(2)}, u32[]{:S(2)}) %collective-permute-start.5) | collective-permute-done | bytes 401440 | tf_op jit(solution)/shard_map/ppermute | solution.py:348
  118.2 0.9 collective-permute-done.6.r3
  119.1 10.0 %collective-permute-done.7.r4 = bf16[784,256]{1,0:T(8,128)(2,1)S(1)} collective-permute-done((bf16[784,256]{1,0:T(8,128)(2,1)}, bf16[784,256]{1,0:T(8,128)(2,1)S(1)}, u32[]{:S(2)}, u32[]{:S(2)}) %collective-permute-start.7) | collective-permute-done | bytes 401440 | tf_op jit(solution)/shard_map/ppermute | solution.py:348
  129.1 2.3 %shard_map.151 = bf16[784,256]{1,0:T(8,128)(2,1)} custom-call(bf16[784,256]{1,0:T(8,128)(2,1)S(1)} %collective-permute-done.4.r0, bf16[784,256]{1,0:T(8,128)(2,1)S(1)} %collective-permute-done.5.r1, bf16[784,256]{1,0:T(8,128)(2,1)S(1)} %get-tuple-element.41.r2, bf16[784,256]{1,0:T(8,128)(2,1)S(1)} %collective-permute-done.6.r3, ...), custom_call_target="tpu_custom_call" | custom-call | bytes 2800000 | tf_op jit(solution)/shard_map/pallas_call | solution.py:59
  131.4 0.6 reshape.136
  132.0 0.7 shard_map.157
  (8 shorter events, 0.1 us)
Async XLA Ops:
  1.3 0.7 copy-start.2
  3.9 16.8 %collective-permute-start.1 = (bf16[800,256]{1,0:T(8,128)(2,1)S(1)}, bf16[800,256]{1,0:T(8,128)(2,1)S(1)}, u32[]{:S(2)}, u32[]{:S(2)}) collective-permute-start(bf16[800,256]{1,0:T(8,128)(2,1)S(1)} %shard_map.146.own_ref), channel_id=1, source_target_pairs={{0,248},{4,252},{8,0},{12,4},{16,8},{20,12},{24,16},{28,20},{32,24... | collective-permute-start | bytes 1228808 | tf_op jit(solution)/shard_map/ppermute | solution.py:348
  12.5 13.4 %collective-permute-start = (bf16[800,256]{1,0:T(8,128)(2,1)S(1)}, bf16[800,256]{1,0:T(8,128)(2,1)S(1)}, u32[]{:S(2)}, u32[]{:S(2)}) collective-permute-start(bf16[800,256]{1,0:T(8,128)(2,1)S(1)} %shard_map.146.own_ref), channel_id=1, source_target_pairs={{0,8},{4,12},{8,16},{12,20},{16,24},{20,28},{24,32},{28,36},{32,40... | collective-permute-start | bytes 1228808 | tf_op jit(solution)/shard_map/ppermute | solution.py:348
  12.5 18.1 %collective-permute-start.2 = (bf16[800,256]{1,0:T(8,128)(2,1)S(1)}, bf16[800,256]{1,0:T(8,128)(2,1)S(1)}, u32[]{:S(2)}, u32[]{:S(2)}) collective-permute-start(bf16[800,256]{1,0:T(8,128)(2,1)S(1)} %shard_map.146.own_ref), channel_id=1, source_target_pairs={{0,4},{4,0},{1,5},{5,1},{2,6},{6,2},{3,7},{7,3},{8,12},{12,8},{9,1... | collective-permute-start | bytes 1228808 | tf_op jit(solution)/shard_map/ppermute | solution.py:352
  26.0 4.6 %collective-permute-start.3 = (bf16[800,256]{1,0:T(8,128)(2,1)S(1)}, bf16[800,256]{1,0:T(8,128)(2,1)S(1)}, u32[]{:S(2)}, u32[]{:S(2)}) collective-permute-start(bf16[800,256]{1,0:T(8,128)(2,1)S(1)} %broadcast_select_fusion), channel_id=1, source_target_pairs={{0,4},{4,0},{1,5},{5,1},{2,6},{6,2},{3,7},{7,3},{8,12},{12,8},{9,1... | collective-permute-start | bytes 1228808 | tf_op jit(solution)/shard_map/ppermute | solution.py:352
  38.2 0.9 copy-start
  39.1 3.1 %collective-permute-start.9 = (bf16[192,1792]{1,0:T(8,128)(2,1)}, bf16[192,1792]{1,0:T(8,128)(2,1)S(1)}, u32[]{:S(2)}, u32[]{:S(2)}) collective-permute-start(bf16[192,1792]{1,0:T(8,128)(2,1)} %get-tuple-element.46.grad_ref), channel_id=1, source_target_pairs={{0,4},{4,0},{1,5},{5,1},{2,6},{6,2},{3,7},{7,3},{8,12},{12,8},{9,1... | collective-permute-start | bytes 2064392 | tf_op jit(solution)/shard_map/ppermute | solution.py:352
  39.1 3.1 %collective-permute-start.8 = (bf16[4,224,192]{2,1,0:T(8,128)(2,1)}, bf16[4,224,192]{2,1,0:T(8,128)(2,1)S(1)}, u32[]{:S(2)}, u32[]{:S(2)}) collective-permute-start(bf16[4,224,192]{2,1,0:T(8,128)(2,1)} %get-tuple-element.45), channel_id=1, source_target_pairs={{0,4},{4,0},{1,5},{5,1},{2,6},{6,2},{3,7},{7,3},{8,12},{12,8},{9,1... | collective-permute-start | bytes 1032200 | tf_op jit(solution)/shard_map/ppermute | solution.py:352
  39.6 2.6 %collective-permute-start.10 = (f32[56,256]{1,0:T(8,128)S(1)}, f32[56,256]{1,0:T(8,128)S(1)}, u32[]{:S(2)}, u32[]{:S(2)}) collective-permute-start(f32[56,256]{1,0:T(8,128)S(1)} %get-tuple-element.48), channel_id=1, source_target_pairs={{0,4},{4,0},{1,5},{5,1},{2,6},{6,2},{3,7},{7,3},{8,12},{12,8},{9,1... | collective-permute-start | bytes 172040 | tf_op jit(solution)/shard_map/ppermute | solution.py:352
  39.6 1.1 copy-start.1
  45.5 19.7 %collective-permute-start.11 = (bf16[248,768]{1,0:T(8,128)(2,1)S(1)}, bf16[248,768]{1,0:T(8,128)(2,1)S(1)}, u32[]{:S(2)}, u32[]{:S(2)}) collective-permute-start(bf16[248,768]{1,0:T(8,128)(2,1)S(1)} %get-tuple-element.50), channel_id=1, source_target_pairs={{0,64},{64,128},{128,192},{192,0},{1,65},{65,129},{129,193},{193,1... | collective-permute-start | bytes 1142792 | tf_op jit(solution)/shard_map/ppermute | solution.py:348
  45.6 29.0 %collective-permute-start.14 = (bf16[4,56,1024]{2,1,0:T(8,128)(2,1)S(1)}, bf16[4,56,1024]{2,1,0:T(8,128)(2,1)S(1)}, u32[]{:S(2)}, u32[]{:S(2)}) collective-permute-start(bf16[4,56,1024]{2,1,0:T(8,128)(2,1)S(1)} %get-tuple-element.54), channel_id=1, source_target_pairs={{0,1},{1,2},{2,3},{3,0},{4,5},{5,6},{6,7},{7,4},{8,9},{9,10},{10,1... | collective-permute-start | bytes 1376264 | tf_op jit(solution)/shard_map/ppermute | solution.py:348
  47.1 27.5 %collective-permute-start.15 = (bf16[4,56,1024]{2,1,0:T(8,128)(2,1)S(1)}, bf16[4,56,1024]{2,1,0:T(8,128)(2,1)S(1)}, u32[]{:S(2)}, u32[]{:S(2)}) collective-permute-start(bf16[4,56,1024]{2,1,0:T(8,128)(2,1)S(1)} %get-tuple-element.55), channel_id=1, source_target_pairs={{0,2},{1,3},{2,0},{3,1},{4,6},{5,7},{6,4},{7,5},{8,10},{9,11},{10,... | collective-permute-start | bytes 1376264 | tf_op jit(solution)/shard_map/ppermute | solution.py:348
  49.8 24.9 %collective-permute-start.16 = (bf16[4,56,1024]{2,1,0:T(8,128)(2,1)S(1)}, bf16[4,56,1024]{2,1,0:T(8,128)(2,1)S(1)}, u32[]{:S(2)}, u32[]{:S(2)}) collective-permute-start(bf16[4,56,1024]{2,1,0:T(8,128)(2,1)S(1)} %get-tuple-element.56), channel_id=1, source_target_pairs={{0,3},{1,0},{2,1},{3,2},{4,7},{5,4},{6,5},{7,6},{8,11},{9,8},{10,9... | collective-permute-start | bytes 1376264 | tf_op jit(solution)/shard_map/ppermute | solution.py:348
  50.8 14.4 %collective-permute-start.12 = (bf16[248,768]{1,0:T(8,128)(2,1)S(1)}, bf16[248,768]{1,0:T(8,128)(2,1)S(1)}, u32[]{:S(2)}, u32[]{:S(2)}) collective-permute-start(bf16[248,768]{1,0:T(8,128)(2,1)S(1)} %get-tuple-element.51), channel_id=1, source_target_pairs={{0,128},{64,192},{128,0},{192,64},{1,129},{65,193},{129,1},{193,65... | collective-permute-start | bytes 1142792 | tf_op jit(solution)/shard_map/ppermute | solution.py:348
  65.2 9.4 %collective-permute-start.13 = (bf16[248,768]{1,0:T(8,128)(2,1)S(1)}, bf16[248,768]{1,0:T(8,128)(2,1)S(1)}, u32[]{:S(2)}, u32[]{:S(2)}) collective-permute-start(bf16[248,768]{1,0:T(8,128)(2,1)S(1)} %get-tuple-element.52), channel_id=1, source_target_pairs={{0,192},{64,0},{128,64},{192,128},{1,193},{65,1},{129,65},{193,129... | collective-permute-start | bytes 1142792 | tf_op jit(solution)/shard_map/ppermute | solution.py:348
  75.9 7.8 %collective-permute-start.20 = (bf16[56,1024]{1,0:T(8,128)(2,1)S(1)}, bf16[56,1024]{1,0:T(8,128)(2,1)S(1)}, u32[]{:S(2)}, u32[]{:S(2)}) collective-permute-start(bf16[56,1024]{1,0:T(8,128)(2,1)S(1)} %get-tuple-element.62), channel_id=1, source_target_pairs={{0,64},{64,128},{128,192},{192,0},{1,65},{65,129},{129,193},{193,1... | collective-permute-start | bytes 344072 | tf_op jit(solution)/shard_map/ppermute | solution.py:348
  76.0 11.7 %collective-permute-start.17 = (bf16[80,768]{1,0:T(8,128)(2,1)S(1)}, bf16[80,768]{1,0:T(8,128)(2,1)S(1)}, u32[]{:S(2)}, u32[]{:S(2)}) collective-permute-start(bf16[80,768]{1,0:T(8,128)(2,1)S(1)} %get-tuple-element.58), channel_id=1, source_target_pairs={{0,1},{1,2},{2,3},{3,0},{4,5},{5,6},{6,7},{7,4},{8,9},{9,10},{10,1... | collective-permute-start | bytes 368648 | tf_op jit(solution)/shard_map/ppermute | solution.py:348
  77.3 10.3 %collective-permute-start.18 = (bf16[80,768]{1,0:T(8,128)(2,1)S(1)}, bf16[80,768]{1,0:T(8,128)(2,1)S(1)}, u32[]{:S(2)}, u32[]{:S(2)}) collective-permute-start(bf16[80,768]{1,0:T(8,128)(2,1)S(1)} %get-tuple-element.59), channel_id=1, source_target_pairs={{0,2},{1,3},{2,0},{3,1},{4,6},{5,7},{6,4},{7,5},{8,10},{9,11},{10,... | collective-permute-start | bytes 368648 | tf_op jit(solution)/shard_map/ppermute | solution.py:348
  80.0 7.7 %collective-permute-start.19 = (bf16[80,768]{1,0:T(8,128)(2,1)S(1)}, bf16[80,768]{1,0:T(8,128)(2,1)S(1)}, u32[]{:S(2)}, u32[]{:S(2)}) collective-permute-start(bf16[80,768]{1,0:T(8,128)(2,1)S(1)} %get-tuple-element.60), channel_id=1, source_target_pairs={{0,3},{1,0},{2,1},{3,2},{4,7},{5,4},{6,5},{7,6},{8,11},{9,8},{10,9... | collective-permute-start | bytes 368648 | tf_op jit(solution)/shard_map/ppermute | solution.py:348
  81.0 5.4 %collective-permute-start.21 = (bf16[56,1024]{1,0:T(8,128)(2,1)S(1)}, bf16[56,1024]{1,0:T(8,128)(2,1)S(1)}, u32[]{:S(2)}, u32[]{:S(2)}) collective-permute-start(bf16[56,1024]{1,0:T(8,128)(2,1)S(1)} %get-tuple-element.63), channel_id=1, source_target_pairs={{0,128},{64,192},{128,0},{192,64},{1,129},{65,193},{129,1},{193,65... | collective-permute-start | bytes 344072 | tf_op jit(solution)/shard_map/ppermute | solution.py:348
  83.6 4.0 %collective-permute-start.22 = (bf16[56,1024]{1,0:T(8,128)(2,1)S(1)}, bf16[56,1024]{1,0:T(8,128)(2,1)S(1)}, u32[]{:S(2)}, u32[]{:S(2)}) collective-permute-start(bf16[56,1024]{1,0:T(8,128)(2,1)S(1)} %get-tuple-element.64), channel_id=1, source_target_pairs={{0,192},{64,0},{128,64},{192,128},{1,193},{65,1},{129,65},{193,129... | collective-permute-start | bytes 344072 | tf_op jit(solution)/shard_map/ppermute | solution.py:348
  88.6 21.7 %all-to-all-start = ((bf16[8,15,1792]{2,1,0:T(8,128)(2,1)}), bf16[8,15,1792]{2,1,0:T(8,128)(2,1)S(1)}, u32[]{:S(2)}, u32[]{:S(2)}) async-start(bf16[8,15,1792]{2,1,0:T(8,128)(2,1)} %shard_map.155), calls=%async_computation | async-start | bytes 917504 | tf_op jit(solution)/shard_map/all_to_all | solution.py:462
  101.2 11.9 %collective-permute-start.4 = (bf16[784,256]{1,0:T(8,128)(2,1)}, bf16[784,256]{1,0:T(8,128)(2,1)S(1)}, u32[]{:S(2)}, u32[]{:S(2)}) collective-permute-start(bf16[784,256]{1,0:T(8,128)(2,1)} %get-tuple-element.39), channel_id=1, source_target_pairs={{0,248},{4,252},{8,0},{12,4},{16,8},{20,12},{24,16},{28,20},{32,24... | collective-permute-start | bytes 1204232 | tf_op jit(solution)/shard_map/ppermute | solution.py:348
  105.7 12.6 %collective-permute-start.5 = (bf16[784,256]{1,0:T(8,128)(2,1)}, bf16[784,256]{1,0:T(8,128)(2,1)S(1)}, u32[]{:S(2)}, u32[]{:S(2)}) collective-permute-start(bf16[784,256]{1,0:T(8,128)(2,1)} %get-tuple-element.40), channel_id=1, source_target_pairs={{0,252},{4,0},{8,4},{12,8},{16,12},{20,16},{24,20},{28,24},{32,28}... | collective-permute-start | bytes 1204232 | tf_op jit(solution)/shard_map/ppermute | solution.py:348
  110.3 8.7 %collective-permute-start.6 = (bf16[784,256]{1,0:T(8,128)(2,1)}, bf16[784,256]{1,0:T(8,128)(2,1)S(1)}, u32[]{:S(2)}, u32[]{:S(2)}) collective-permute-start(bf16[784,256]{1,0:T(8,128)(2,1)} %get-tuple-element.42), channel_id=1, source_target_pairs={{0,4},{4,8},{8,12},{12,16},{16,20},{20,24},{24,28},{28,32},{32,36}... | collective-permute-start | bytes 1204232 | tf_op jit(solution)/shard_map/ppermute | solution.py:348
  110.3 18.7 %collective-permute-start.7 = (bf16[784,256]{1,0:T(8,128)(2,1)}, bf16[784,256]{1,0:T(8,128)(2,1)S(1)}, u32[]{:S(2)}, u32[]{:S(2)}) collective-permute-start(bf16[784,256]{1,0:T(8,128)(2,1)} %get-tuple-element.43), channel_id=1, source_target_pairs={{0,8},{4,12},{8,16},{12,20},{16,24},{20,28},{24,32},{28,36},{32,40... | collective-permute-start | bytes 1204232 | tf_op jit(solution)/shard_map/ppermute | solution.py:348
  110.4 21.6 %collective-permute-start.23 = (f32[56,256]{1,0:T(8,128)S(1)}, f32[56,256]{1,0:T(8,128)S(1)}, u32[]{:S(2)}, u32[]{:S(2)}) collective-permute-start(f32[56,256]{1,0:T(8,128)S(1)} %get-tuple-element.66.mine_ref), channel_id=1, source_target_pairs={{0,4},{4,0},{1,5},{5,1},{2,6},{6,2},{3,7},{7,3},{8,12},{12,8},{9,1... | collective-permute-start | bytes 172040 | tf_op jit(solution)/shard_map/ppermute | solution.py:352
